TPU v7x, 32 devices: a whole 2x2x4 slice. The times are simulated.
32 devices in a mesh: fsdp: 8 (over z, y), seq: 4 (over x, core).
Axes of the slice: x: 2, y: 2, z: 4, core: 2. Of those that a mesh axis runs over, the one named last changes fastest.
Arguments:
- tokens: bfloat16 [16, 1024, 1024], P('fsdp', 'seq'), may hold values from -6 to 6
- first_gain: float32 [1024], replicated, may hold values from 0.5 to 1.5
- first_shift: float32 [1024], replicated, may hold values from -1 to 1
- attention_weight: bfloat16 [1024, 3072], P('fsdp', 'seq'), may hold values from -0.25 to 0.25
- attention_bias: float32 [3072], replicated, may hold values from -1.5 to 1.5
- output_weight: bfloat16 [1024, 1024], P('fsdp', 'seq'), may hold values from -1.5 to 1.5
- output_bias: float32 [1024], replicated, may hold values from -1 to 1
- second_gain: float32 [1024], replicated, may hold values from 0.5 to 1.5
- second_shift: float32 [1024], replicated, may hold values from -1 to 1
- expand_weight: bfloat16 [1024, 4096], P('fsdp', 'seq'), may hold values from -0.1875 to 0.1875
- expand_bias: float32 [4096], replicated, may hold values from -1 to 1
- contract_weight: bfloat16 [4096, 1024], P('fsdp', 'seq'), may hold values from -0.1875 to 0.1875
- contract_bias: float32 [1024], replicated, may hold values from -1 to 1
- cotangent: bfloat16 [16, 1024, 1024], P('fsdp', 'seq'), may hold values from -6 to 6
- threshold: float32 [1], replicated, may hold values from 3 to 6
Outputs:
- block_output: bfloat16 [16, 1024, 1024], P('fsdp', 'seq')
- input_grad: float32 [16, 1024, 1024], P('fsdp', 'seq')
- grad_first_gain: float32 [1024], replicated
- grad_first_shift: float32 [1024], replicated
- grad_attention_weight: float32 [1024, 3072], P('fsdp', 'seq')
- grad_attention_bias: float32 [3072], replicated
- grad_output_weight: float32 [1024, 1024], P('fsdp', 'seq')
- grad_output_bias: float32 [1024], replicated
- grad_second_gain: float32 [1024], replicated
- grad_second_shift: float32 [1024], replicated
- grad_expand_weight: float32 [1024, 4096], P('fsdp', 'seq')
- grad_expand_bias: float32 [4096], replicated
- grad_contract_weight: float32 [4096, 1024], P('fsdp', 'seq')
- grad_contract_bias: float32 [1024], replicated
- head_peak: float32 [16], P('seq')
- clipped_weight: float32 [1024, 3072], P('fsdp', 'seq')
- clipped_bias: float32 [3072], P('seq')
All inputs are finite; a program needn't handle non-finite values.
Results may differ from a plain program's by a relative error of at most 0.018.
Values may be sent and summed in bfloat16 or wider, within the bound.
No kernel may reach another device: no remote copies, remote signals or barrier semaphores. Data moves between devices by JAX's collectives and lax.ppermute only.
A program may use at most 320 MiB of HBM per device.

v0:
```python
import jax
import jax.numpy as jnp
from jax import lax
from jax.sharding import PartitionSpec as P

D = 1024
H = 16
HD = 64
QBLK = 512


def layer_norm(values, gain, shift):
    centered = values - jnp.mean(values, axis=-1, keepdims=True)
    variance = jnp.mean(centered * centered, axis=-1, keepdims=True)
    return centered * lax.rsqrt(variance + 1e-05) * gain + shift


def gelu_tanh(values):
    return jax.nn.gelu(values, approximate=True)


def causal_mask(row_start, row_stop):
    row_ids = row_start + jnp.arange(row_stop - row_start)[:, None]
    col_ids = jnp.arange(row_stop)[None, :]
    return col_ids <= row_ids


def block_logits(query_block, keys_part, row_start, row_stop, logit_scale):
    logits = (
        jnp.einsum("nqhd,nkhd->nhqk", query_block, keys_part, preferred_element_type=jnp.float32)
        * logit_scale
    )
    return jnp.where(causal_mask(row_start, row_stop), logits, -jnp.inf)


def split_packed(packed):
    head_size = packed.shape[-1] // 3
    return (
        packed[..., :head_size],
        packed[..., head_size : 2 * head_size],
        packed[..., 2 * head_size :],
    )


def attend_forward(packed):
    queries, keys_all, values_all = split_packed(packed)
    length = packed.shape[1]
    logit_scale = queries.shape[-1] ** (-0.5)
    outputs = []
    log_sums = []
    peak_value = None
    for block_index in range(length // QBLK):
        row_start = block_index * QBLK
        row_stop = row_start + QBLK
        logits = block_logits(
            queries[:, row_start:row_stop], keys_all[:, :row_stop], row_start, row_stop, logit_scale
        )
        row_top = jnp.max(logits, axis=-1, keepdims=True)
        shifted = jnp.exp(logits - row_top)
        row_total = jnp.sum(shifted, axis=-1, keepdims=True)
        probabilities = (shifted / row_total).astype(jnp.bfloat16)
        block_out = jnp.einsum(
            "nhqk,nkhd->nqhd",
            probabilities,
            values_all[:, :row_stop],
            preferred_element_type=jnp.float32,
        )
        outputs.append(block_out.astype(jnp.bfloat16))
        log_sums.append((row_top + jnp.log(row_total))[..., 0])
        block_peak = jnp.max(row_top[..., 0], axis=-1)
        peak_value = block_peak if peak_value is None else jnp.maximum(peak_value, block_peak)
    return (jnp.concatenate(outputs, axis=1), jnp.concatenate(log_sums, axis=-1), peak_value)


def attend_items(packed):
    attended, log_sums, peak_value = attend_forward(packed)
    returned = lax.all_to_all(attended, "seq", split_axis=1, concat_axis=2, tiled=True)
    return (returned, log_sums, peak_value, packed)


def attend_backward(packed, log_sums, heads_cot):
    queries, keys_all, values_all = split_packed(packed)
    length = packed.shape[1]
    logit_scale = queries.shape[-1] ** (-0.5)
    query_grads = []
    key_grad = jnp.zeros(keys_all.shape, jnp.float32)
    value_grad = jnp.zeros(values_all.shape, jnp.float32)
    for block_index in range(length // QBLK):
        row_start = block_index * QBLK
        row_stop = row_start + QBLK
        query_block = queries[:, row_start:row_stop]
        cot_block = heads_cot[:, row_start:row_stop]
        logits = block_logits(query_block, keys_all[:, :row_stop], row_start, row_stop, logit_scale)
        probabilities = jnp.exp(logits - log_sums[:, :, row_start:row_stop, None])
        prob_grad = jnp.einsum(
            "nqhd,nkhd->nhqk",
            cot_block,
            values_all[:, :row_stop],
            preferred_element_type=jnp.float32,
        )
        row_inner = jnp.sum(prob_grad * probabilities, axis=-1, keepdims=True)
        logit_grad = (probabilities * (prob_grad - row_inner)).astype(jnp.bfloat16)
        query_grads.append(
            jnp.einsum(
                "nhqk,nkhd->nqhd",
                logit_grad,
                keys_all[:, :row_stop],
                preferred_element_type=jnp.float32,
            )
            * logit_scale
        )
        key_grad = key_grad.at[:, :row_stop].add(
            jnp.einsum(
                "nhqk,nqhd->nkhd", logit_grad, query_block, preferred_element_type=jnp.float32
            )
            * logit_scale
        )
        value_grad = value_grad.at[:, :row_stop].add(
            jnp.einsum(
                "nhqk,nqhd->nkhd",
                probabilities.astype(jnp.bfloat16),
                cot_block,
                preferred_element_type=jnp.float32,
            )
        )
    joined = jnp.concatenate([jnp.concatenate(query_grads, axis=1), key_grad, value_grad], axis=-1)
    return joined.astype(jnp.bfloat16)


def body(
    tokens,
    first_gain,
    first_shift,
    attention_weight,
    attention_bias,
    output_weight,
    output_bias,
    second_gain,
    second_shift,
    expand_weight,
    expand_bias,
    contract_weight,
    contract_bias,
    cotangent,
    threshold,
):
    partial_full = (
        lax.all_gather(attention_weight, "seq", axis=1, tiled=True),
        lax.all_gather(output_weight, "seq", axis=1, tiled=True),
        lax.all_gather(expand_weight, "seq", axis=1, tiled=True),
        lax.all_gather(contract_weight, "seq", axis=1, tiled=True),
    )
    full_weights = (
        lax.all_gather(partial_full[0], "fsdp", axis=0, tiled=True),
        lax.all_gather(partial_full[1], "fsdp", axis=0, tiled=True),
        lax.all_gather(partial_full[2], "fsdp", axis=0, tiled=True),
        lax.all_gather(partial_full[3], "fsdp", axis=0, tiled=True),
    )
    mixing_full, output_full, expand_full, contract_full = full_weights
    seq_here = tokens.shape[0]
    tok_here = tokens.shape[1]
    tokens_float = tokens.astype(jnp.float32)
    normed_first = layer_norm(tokens_float, first_gain, first_shift).astype(jnp.bfloat16)
    mixed = (
        jnp.einsum("ntd,de->nte", normed_first, mixing_full, preferred_element_type=jnp.float32)
        + attention_bias
    )
    mixed = mixed.astype(jnp.bfloat16).reshape(seq_here, tok_here, H, 3 * HD)
    returned, log_sums, peaks, packed = attend_items(
        lax.all_to_all(mixed, "seq", split_axis=2, concat_axis=1, tiled=True)
    )
    attended = returned.reshape(seq_here, tok_here, D)
    residual = (
        tokens_float
        + jnp.einsum("nte,ed->ntd", attended, output_full, preferred_element_type=jnp.float32)
        + output_bias
    )
    normed_second = layer_norm(residual, second_gain, second_shift).astype(jnp.bfloat16)
    hidden = (
        jnp.einsum("ntd,di->nti", normed_second, expand_full, preferred_element_type=jnp.float32)
        + expand_bias
    )
    active = gelu_tanh(hidden).astype(jnp.bfloat16)
    result = (
        residual
        + jnp.einsum("nti,id->ntd", active, contract_full, preferred_element_type=jnp.float32)
        + contract_bias
    )
    block_output = result.astype(jnp.bfloat16)
    cot_float = cotangent.astype(jnp.float32)
    grad_contract = jnp.einsum("nti,ntd->id", active, cotangent, preferred_element_type=jnp.float32)
    grad_contract_bias = jnp.sum(cot_float, axis=(0, 1))
    active_cot = jnp.einsum(
        "ntd,id->nti", cotangent, contract_full, preferred_element_type=jnp.float32
    )
    _, gelu_pull = jax.vjp(gelu_tanh, hidden)
    hidden_cot = gelu_pull(active_cot)[0].astype(jnp.bfloat16)
    grad_expand = jnp.einsum(
        "ntd,nti->di", normed_second, hidden_cot, preferred_element_type=jnp.float32
    )
    grad_expand_bias = jnp.sum(hidden_cot.astype(jnp.float32), axis=(0, 1))
    second_cot = jnp.einsum(
        "nti,di->ntd", hidden_cot, expand_full, preferred_element_type=jnp.float32
    )
    _, second_pull = jax.vjp(layer_norm, residual, second_gain, second_shift)
    residual_part, grad_second_gain, grad_second_shift = second_pull(second_cot)
    residual_cot = cot_float + residual_part
    branch_cot = residual_cot.astype(jnp.bfloat16)
    grad_output = jnp.einsum(
        "nte,ntd->ed", attended, branch_cot, preferred_element_type=jnp.float32
    )
    grad_output_bias = jnp.sum(branch_cot.astype(jnp.float32), axis=(0, 1))
    attended_cot = jnp.einsum(
        "ntd,ed->nte", branch_cot, output_full, preferred_element_type=jnp.float32
    )
    attended_cot = attended_cot.astype(jnp.bfloat16).reshape(seq_here, tok_here, H, HD)
    heads_cot = lax.all_to_all(attended_cot, "seq", split_axis=2, concat_axis=1, tiled=True)
    packed_cot = attend_backward(packed, log_sums, heads_cot)
    mixed_cot = lax.all_to_all(packed_cot, "seq", split_axis=1, concat_axis=2, tiled=True).reshape(
        seq_here, tok_here, 3 * D
    )
    grad_mixing = jnp.einsum(
        "ntd,nte->de", normed_first, mixed_cot, preferred_element_type=jnp.float32
    )
    grad_mixing_bias = jnp.sum(mixed_cot.astype(jnp.float32), axis=(0, 1))
    first_cot = jnp.einsum(
        "nte,de->ntd", mixed_cot, mixing_full, preferred_element_type=jnp.float32
    )
    _, first_pull = jax.vjp(layer_norm, tokens_float, first_gain, first_shift)
    token_part, grad_first_gain, grad_first_shift = first_pull(first_cot)
    input_grad = residual_cot + token_part
    summed_first = (
        lax.psum_scatter(
            grad_mixing.astype(jnp.bfloat16), "fsdp", scatter_dimension=0, tiled=True
        ).astype(jnp.float32),
        lax.psum_scatter(
            grad_output.astype(jnp.bfloat16), "fsdp", scatter_dimension=0, tiled=True
        ).astype(jnp.float32),
        lax.psum_scatter(
            grad_expand.astype(jnp.bfloat16), "fsdp", scatter_dimension=0, tiled=True
        ).astype(jnp.float32),
        lax.psum_scatter(
            grad_contract.astype(jnp.bfloat16), "fsdp", scatter_dimension=0, tiled=True
        ).astype(jnp.float32),
    )
    weight_grads = (
        lax.psum_scatter(
            summed_first[0].astype(jnp.bfloat16), "seq", scatter_dimension=1, tiled=True
        ).astype(jnp.float32),
        lax.psum_scatter(
            summed_first[1].astype(jnp.bfloat16), "seq", scatter_dimension=1, tiled=True
        ).astype(jnp.float32),
        lax.psum_scatter(
            summed_first[2].astype(jnp.bfloat16), "seq", scatter_dimension=1, tiled=True
        ).astype(jnp.float32),
        lax.psum_scatter(
            summed_first[3].astype(jnp.bfloat16), "seq", scatter_dimension=1, tiled=True
        ).astype(jnp.float32),
    )
    vector_totals = lax.psum(
        (
            grad_first_gain,
            grad_first_shift,
            grad_mixing_bias,
            grad_output_bias,
            grad_second_gain,
            grad_second_shift,
            grad_expand_bias,
            grad_contract_bias,
        ),
        ("fsdp", "seq"),
    )
    head_peak = lax.pmax(jnp.max(peaks, axis=0), "fsdp")
    rows_here = attention_weight.shape[0]
    col_width = attention_weight.shape[1]
    heads_here = head_peak.shape[0]
    head_size = col_width // (3 * heads_here)
    factor = jnp.sqrt(threshold[0] / jnp.maximum(head_peak, threshold[0]))
    multiplier = jnp.stack([factor, factor, jnp.ones_like(factor)], axis=1)
    clipped_weight = (
        attention_weight.astype(jnp.float32).reshape(rows_here, heads_here, 3, head_size)
        * multiplier[None, :, :, None]
    ).reshape(rows_here, col_width)
    bias_piece = lax.dynamic_slice_in_dim(
        attention_bias, lax.axis_index("seq") * col_width, col_width
    )
    clipped_bias = (bias_piece.reshape(heads_here, 3, head_size) * multiplier[:, :, None]).reshape(
        col_width
    )
    return (
        block_output,
        input_grad,
        vector_totals[0],
        vector_totals[1],
        weight_grads[0],
        vector_totals[2],
        weight_grads[1],
        vector_totals[3],
        vector_totals[4],
        vector_totals[5],
        weight_grads[2],
        vector_totals[6],
        weight_grads[3],
        vector_totals[7],
        head_peak,
        clipped_weight,
        clipped_bias,
    )


def solution(mesh):
    placed = (
        P("fsdp", "seq", None),
        P(),
        P(),
        P("fsdp", "seq"),
        P(),
        P("fsdp", "seq"),
        P(),
        P(),
        P(),
        P("fsdp", "seq"),
        P(),
        P("fsdp", "seq"),
        P(),
        P("fsdp", "seq", None),
        P(),
    )
    return jax.shard_map(
        body,
        mesh=mesh,
        in_specs=placed,
        out_specs=(
            P("fsdp", "seq", None),
            P("fsdp", "seq", None),
            P(),
            P(),
            P("fsdp", "seq"),
            P(),
            P("fsdp", "seq"),
            P(),
            P(),
            P(),
            P("fsdp", "seq"),
            P(),
            P("fsdp", "seq"),
            P(),
            P("seq"),
            P("fsdp", "seq"),
            P("seq"),
        ),
        check_vma=False,
    )
```

profile of v0, /device:TPU:0, one launch (start us, length us, event | category | flops | bytes accessed | tf_op | source)
XLA Modules:
  0.0 1167.2 jit_solution(12801582693143362905)
XLA Ops:
  8.8 11.7 %all_gather.24 = bf16[128,3072]{1,0:T(8,128)(2,1)} all-gather(bf16[128,768]{1,0:T(8,128)(2,1)} %param.30), channel_id=1, replica_groups=mesh['fsdp'=8,'seq'=4] {'seq'}, dimensions={1}, use_global_device_ids=true | all-gather | bytes 983040 | tf_op jit(solution)/shard_map/all_gather | solution.py:148
  20.5 8.3 all_gather.26
  30.6 18.4 %all-gather.15.cloned.1.call-done = bf16[512,1024]{1,0:T(8,128)(2,1)} async-done(((bf16[512,256]{1,0:T(8,128)(2,1)}), bf16[512,1024]{1,0:T(8,128)(2,1)}) %all-gather.15.cloned.1.call-update) | async-done | bytes 1048592 | tf_op jit(solution)/shard_map/all_gather | solution.py:151
  49.6 100.5 %all-gather.7.cloned.1.call-done = bf16[1024,3072]{1,0:T(8,128)(2,1)} async-done(((bf16[128,3072]{1,0:T(8,128)(2,1)}), bf16[1024,3072]{1,0:T(8,128)(2,1)}) %all-gather.7.cloned.1.call-update) | async-done | bytes 6291472 | tf_op jit(solution)/shard_map/all_gather | solution.py:154
  150.2 7.8 add_convert_fusion
  158.0 4.7 copy.155
  162.8 4.0 copy.156
  166.7 5.0 all-to-all-start
  172.2 36.5 %all-to-all-done = bf16[2,256,16,192]{1,3,0,2:T(8,128)(2,1)} async-done(((bf16[2,256,16,192]{1,3,0,2:T(8,128)(2,1)}), bf16[2,256,16,192]{1,3,0,2:T(8,128)(2,1)}, u32[]{:S(2)}, u32[]{:S(2)}) %all-to-all-start) | async-done | bytes 3145760 | tf_op jit(solution)/shard_map/all_to_all | solution.py:170
  208.7 6.3 copy.158
  215.0 6.1 all_to_all.51
  221.1 2.7 fusion.104
  225.0 3.1 copy-done.7
  228.0 3.0 fusion.103
  231.1 3.7 fusion
  236.8 4.5 fusion.73
  242.4 2.9 copy.160
  245.3 2.7 reshape.309
  248.0 18.9 %all_to_all.66 = bf16[4,2,65536]{2,1,0:T(2,128)(2,1)} all-to-all(bf16[4,2,65536]{2,1,0:T(2,128)(2,1)} %reshape.309), channel_id=1, replica_groups=mesh['fsdp'=8,'seq'=4] {'seq'}, dimensions={0} | all-to-all | bytes 2097152 | tf_op jit(solution)/shard_map/all_to_all | solution.py:77
  266.9 3.1 reshape.310
  270.0 2.6 copy.162
  272.6 3.3 fusion.105
  276.3 48.9 %all-gather.13.cloned.1.call-done = bf16[1024,4096]{1,0:T(8,128)(2,1)} async-done(((bf16[128,4096]{1,0:T(8,128)(2,1)}), bf16[1024,4096]{1,0:T(8,128)(2,1)}) %all-gather.13.cloned.1.call-update) | async-done | bytes 8388624 | tf_op jit(solution)/shard_map/all_gather | solution.py:156
  325.2 10.2 fusion.17
  335.4 114.9 %all-gather.17.cloned.1.call-done = bf16[4096,1024]{1,0:T(8,128)(2,1)} async-done(((bf16[512,1024]{1,0:T(8,128)(2,1)}), bf16[4096,1024]{1,0:T(8,128)(2,1)}) %all-gather.17.cloned.1.call-update) | async-done | bytes 8388624 | tf_op jit(solution)/shard_map/all_gather | solution.py:157
  450.4 14.6 %convert_reduce_fusion = (f32[4096]{0:T(1024)}, bf16[2,256,4096]{2,1,0:T(8,128)(2,1)S(1)}) fusion(f32[2,256,4096]{2,1,0:T(8,128)} %fusion.17, f32[4096]{0:T(1024)S(1)} %copy-done.41, bf16[2,256,1024]{2,1,0:T(8,128)(2,1)} %param.40, bf16[4096,1024]{1,0:T(8,128)(2,1)} %all-gather.17.cloned.1.call-done), kind=kOutput, calls=%fused_computation.29 | convolution fusion | flops 4343197696 | bytes 22052864 | tf_op jit(solution)/shard_map/ntd,id->nti/dot_general | solution.py:193
  465.0 5.5 multiply_reduce_fusion.2
  473.8 2.3 fusion.57
  478.8 3.5 all-to-all-start.2
  483.0 3.8 bitcast_convert_fusion.3
  486.9 9.9 all-to-all-done.2
  496.7 1.8 copy.196
  498.5 1.9 all_to_all.58
  500.5 6.3 fusion.62
  506.7 7.6 fusion.99
  514.4 4.9 multiply_convert_fusion.1
  519.3 3.5 fusion.71
  522.8 3.4 fusion.65
  526.2 10.9 fusion.98
  537.1 7.9 multiply_convert_fusion
  545.0 4.7 fusion.72
  549.7 4.0 fusion.48
  553.8 4.4 fusion.47
  558.2 1.8 pad_maximum_fusion
  560.0 7.6 copy.170
  567.6 53.8 %all_to_all.67 = bf16[2,1024,4,192]{3,2,0,1:T(4,128)(2,1)} all-to-all(bf16[2,1024,4,192]{3,2,0,1:T(4,128)(2,1)} %copy.170), channel_id=1, replica_groups=mesh['fsdp'=8,'seq'=4] {'seq'}, dimensions={1} | all-to-all | bytes 6291456 | tf_op jit(solution)/shard_map/all_to_all | solution.py:219
  621.5 7.3 copy.172
  628.7 7.7 bitcast_convert_fusion.2
  637.7 13.1 %bitcast_convert_fusion = bf16[4096,1024]{1,0:T(8,128)(2,1)} fusion(bf16[2,256,1024]{2,1,0:T(8,128)(2,1)S(1)} %copy-done.12, f32[2,256,4096]{2,1,0:T(8,128)} %fusion.17, f32[4096]{0:T(1024)S(1)} %copy-done.42), kind=kOutput, calls=%fused_computation | convolution fusion | flops 4320133120 | bytes 17842176 | tf_op jit(solution)/shard_map/nti,ntd->id/dot_general | solution.py:191
  652.4 9.5 bitcast_convert_fusion.1
  662.7 89.2 %reduce-scatter.9.cloned.1.call-done = bf16[128,3072]{1,0:T(8,128)(2,1)} async-done(((bf16[1024,3072]{1,0:T(8,128)(2,1)}), bf16[128,3072]{1,0:T(8,128)(2,1)}) %reduce-scatter.9.cloned.1.call-update) | async-done | bytes 786448 | tf_op jit(solution)/shard_map/reduce_scatter | solution.py:233
  752.7 151.0 %reduce-scatter.21.cloned.1.call-done = bf16[512,1024]{1,0:T(8,128)(2,1)} async-done(((bf16[4096,1024]{1,0:T(8,128)(2,1)}), bf16[512,1024]{1,0:T(8,128)(2,1)}) %reduce-scatter.21.cloned.1.call-update) | async-done | bytes 1048592 | tf_op jit(solution)/shard_map/reduce_scatter | solution.py:242
  903.8 12.2 %add_convert_fusion.1 = bf16[2,256,1024]{2,1,0:T(8,128)(2,1)} fusion(f32[2,256,1024]{2,1,0:T(8,128)S(1)} %copy-done.6, bf16[4096,1024]{1,0:T(8,128)(2,1)} %all-gather.17.cloned.1.call-done, f32[1024]{0:T(1024)S(1)} %copy-done.47, f32[2,256,4096]{2,1,0:T(8,128)} %fusion.17, f32[4096]{0:T(1024)S(1)} %copy-done.42), kind=kOutput, calls=%fused_computation.83 | convolution fusion | flops 4317511680 | bytes 19943424 | tf_op jit(solution)/shard_map/nti,id->ntd/dot_general | solution.py:186
  916.0 20.6 %pmax.7 = f32[4]{0:T(128)S(1)} all-reduce(f32[4]{0:T(128)S(1)} %maximum_reduce_fusion), channel_id=1, replica_groups=mesh['fsdp'=8,'seq'=4] {'fsdp'}, use_global_device_ids=true, to_apply=%region_41.42 | all-reduce | flops 4 | bytes 32 | tf_op jit(solution)/shard_map/pmax | solution.py:273
  939.2 8.0 copy.193
  947.1 3.3 convert_reduce_fusion.1
  950.7 105.3 %reduce-scatter.17.cloned.1.call-done = bf16[128,4096]{1,0:T(8,128)(2,1)} async-done(((bf16[1024,4096]{1,0:T(8,128)(2,1)}), bf16[128,4096]{1,0:T(8,128)(2,1)}) %reduce-scatter.17.cloned.1.call-update) | async-done | bytes 1048592 | tf_op jit(solution)/shard_map/reduce_scatter | solution.py:239
  1056.0 7.0 fusion.100
  1064.6 2.1 convert_reduce_fusion.3
  1066.7 40.8 %all-reduce.2 = (f32[1024]{0:T(1024)}, f32[1024]{0:T(1024)}, f32[3072]{0:T(1024)}, f32[1024]{0:T(1024)}, f32[1024]{0:T(1024)}, /*index=5*/f32[1024]{0:T(1024)}, f32[4096]{0:T(1024)}, f32[1024]{0:T(1024)}) all-reduce(f32[1024]{0:T(1024)S(1)} %get-tuple-element.87, ...), channel_id=1, replica_groups=mesh['fsdp'=8,'seq'=4] {'fsdp','seq'}, use_global_device_ids=true, to_apply=%region_15.16 | all-reduce | flops 13312 | bytes 106496 | tf_op jit(solution)/shard_map/psum | solution.py:260
  1110.7 20.5 %reduce-scatter.23.cloned.1.call-done = bf16[512,256]{1,0:T(8,128)(2,1)} async-done(((bf16[512,1024]{1,0:T(8,128)(2,1)}), bf16[512,256]{1,0:T(8,128)(2,1)}) %reduce-scatter.23.cloned.1.call-update) | async-done | bytes 262160 | tf_op jit(solution)/shard_map/reduce_scatter | solution.py:256
  1131.2 1.8 convert_element_type.136
  1133.0 25.7 %reduce-scatter.19.cloned.1.call-done = bf16[128,1024]{1,0:T(8,128)(2,1)} async-done(((bf16[128,4096]{1,0:T(8,128)(2,1)}), bf16[128,1024]{1,0:T(8,128)(2,1)}) %reduce-scatter.19.cloned.1.call-update) | async-done | bytes 262160 | tf_op jit(solution)/shard_map/reduce_scatter | solution.py:253
  1158.7 1.8 convert_element_type.133
  (183 shorter events, 27.2 us)
Async XLA Ops:
  7.2 41.8 %copy-start.2 = (bf16[2,256,1024]{2,1,0:T(8,128)(2,1)S(1)}, bf16[2,256,1024]{2,1,0:T(8,128)(2,1)}, u32[]{:S(2)}) copy-start(bf16[2,256,1024]{2,1,0:T(8,128)(2,1)} %param.27) | copy-start | bytes 3145732
  7.2 143.0 %copy-start.28 = (f32[1024]{0:T(1024)S(1)}, f32[1024]{0:T(1024)}, u32[]{:S(2)}) copy-start(f32[1024]{0:T(1024)} %param.28) | copy-start | bytes 12292
  7.2 143.0 %copy-start.39 = (f32[3072]{0:T(1024)S(1)}, f32[3072]{0:T(1024)}, u32[]{:S(2)}) copy-start(f32[3072]{0:T(1024)} %param.31) | copy-start | bytes 36868
  7.2 143.0 %copy-start.43 = (f32[1024]{0:T(1024)S(1)}, f32[1024]{0:T(1024)}, u32[]{:S(2)}) copy-start(f32[1024]{0:T(1024)} %param.29) | copy-start | bytes 12292
  7.2 23.3 %all-gather.11.cloned.1.call-start = ((), (), s32[]{:S(2)}) async-start(), calls=%async_computation.14 | async-start | bytes 1310720 | tf_op jit(solution)/shard_map/all_gather | solution.py:150
  8.0 41.0 %all-gather.15.cloned.1.call-start = ((), (), s32[]{:S(2)}) async-start(), calls=%async_computation.16 | async-start | bytes 1310720 | tf_op jit(solution)/shard_map/all_gather | solution.py:151
  8.7 141.5 %all-gather.7.cloned.1.call-start = ((), (), s32[]{:S(2)}) async-start(), calls=%async_computation.12 | async-start | bytes 7077888 | tf_op jit(solution)/shard_map/all_gather | solution.py:154
  20.5 252.2 %all-gather.9.cloned.1.call-start = ((), (), s32[]{:S(2)}) async-start(), calls=%async_computation.13 | async-start | bytes 2359296 | tf_op jit(solution)/shard_map/all_gather | solution.py:155
  28.9 296.4 %all-gather.13.cloned.1.call-start = ((), (), s32[]{:S(2)}) async-start(), calls=%async_computation.15 | async-start | bytes 9437184 | tf_op jit(solution)/shard_map/all_gather | solution.py:156
  30.5 419.8 %all-gather.17.cloned.1.call-start = ((), (), s32[]{:S(2)}) async-start(), calls=%async_computation.17 | async-start | bytes 9437184 | tf_op jit(solution)/shard_map/all_gather | solution.py:157
  49.2 108.8 %copy-start.21 = (f32[2,256]{1,0:T(2,128)}, f32[2,256]{1,0:T(2,128)S(1)}, u32[]{:S(2)}) copy-start(f32[2,256]{1,0:T(2,128)S(1)} %broadcast_multiply_fusion.1) | copy-start | bytes 6148
  49.6 108.4 %copy-start.25 = (f32[2,256]{1,0:T(2,128)}, f32[2,256]{1,0:T(2,128)S(1)}, u32[]{:S(2)}) copy-start(f32[2,256]{1,0:T(2,128)S(1)} %fusion.44) | copy-start | bytes 6148
  49.6 108.4 %copy-start.23 = (f32[2,256]{1,0:T(2,128)}, f32[2,256]{1,0:T(2,128)S(1)}, u32[]{:S(2)}) copy-start(f32[2,256]{1,0:T(2,128)S(1)} %fusion.96) | copy-start | bytes 6148
  166.7 42.0 %all-to-all-start = ((bf16[2,256,16,192]{1,3,0,2:T(8,128)(2,1)}), bf16[2,256,16,192]{1,3,0,2:T(8,128)(2,1)}, u32[]{:S(2)}, u32[]{:S(2)}) async-start(bf16[2,256,16,192]{1,3,0,2:T(8,128)(2,1)} %copy.156), calls=%async_computation | async-start | bytes 6291456 | tf_op jit(solution)/shard_map/all_to_all | solution.py:170
  223.8 11.0 copy-start.1
  223.8 4.3 copy-start.7
  231.0 5.7 copy-start
  248.0 24.6 %copy-start.27 = (f32[1024]{0:T(1024)S(1)}, f32[1024]{0:T(1024)}, u32[]{:S(2)}) copy-start(f32[1024]{0:T(1024)} %param.33) | copy-start | bytes 12292
  272.6 52.6 %copy-start.37 = (f32[1024]{0:T(1024)S(1)}, f32[1024]{0:T(1024)}, u32[]{:S(2)}) copy-start(f32[1024]{0:T(1024)} %param.34) | copy-start | bytes 12292
  272.6 52.6 %copy-start.45 = (f32[1024]{0:T(1024)S(1)}, f32[1024]{0:T(1024)}, u32[]{:S(2)}) copy-start(f32[1024]{0:T(1024)} %param.35) | copy-start | bytes 12292
  275.9 194.5 %copy-start.5 = (f32[2,256,1024]{2,1,0:T(8,128)}, f32[2,256,1024]{2,1,0:T(8,128)S(1)}, u32[]{:S(2)}) copy-start(f32[2,256,1024]{2,1,0:T(8,128)S(1)} %get-tuple-element.111) | copy-start | bytes 6291460
  276.3 194.1 %copy-start.31 = (f32[2,256]{1,0:T(2,128)}, f32[2,256]{1,0:T(2,128)S(1)}, u32[]{:S(2)}) copy-start(f32[2,256]{1,0:T(2,128)S(1)} %fusion.97) | copy-start | bytes 6148
  276.3 174.0 %copy-start.41 = (f32[4096]{0:T(1024)S(1)}, f32[4096]{0:T(1024)}, u32[]{:S(2)}) copy-start(f32[4096]{0:T(1024)} %param.37) | copy-start | bytes 49156
  450.4 14.6 %copy-start.40 = (bf16[1024,4096]{1,0:T(8,128)(2,1)S(1)}, bf16[1024,4096]{1,0:T(8,128)(2,1)}, u32[]{:S(2)}) copy-start(bf16[1024,4096]{1,0:T(8,128)(2,1)} %all-gather.13.cloned.1.call-done) | copy-start | bytes 25165828
  464.9 5.5 copy-start.49
  470.4 2.0 copy-start.11
  470.5 3.4 copy-start.15
  476.1 6.8 copy-start.14
  478.8 18.0 %all-to-all-start.2 = ((bf16[2,256,16,64]{1,3,0,2:T(8,128)(2,1)}), bf16[2,256,16,64]{1,3,0,2:T(8,128)(2,1)S(1)}, u32[]{:S(2)}, u32[]{:S(2)}) async-start(bf16[2,256,16,64]{1,3,0,2:T(8,128)(2,1)} %copy.165), calls=%async_computation.2 | async-start | bytes 2097152 | tf_op jit(solution)/shard_map/all_to_all | solution.py:217
  482.3 179.7 %reduce-scatter.13.cloned.1.call-start = ((), (), s32[]{:S(2)}) async-start(), calls=%async_computation.20 | async-start | bytes 2359296 | tf_op jit(solution)/shard_map/reduce_scatter | solution.py:236
  486.8 265.1 %reduce-scatter.9.cloned.1.call-start = ((), (), s32[]{:S(2)}) async-start(), calls=%async_computation.18 | async-start | bytes 7077888 | tf_op jit(solution)/shard_map/reduce_scatter | solution.py:233
  500.5 6.3 copy-start.8
  500.5 13.9 %slice-start.4 = ((s8[8388608]{0:T(1024)(128)(4,1)}), s8[4194304]{0:T(1024)(128)(4,1)S(1)}, s32[]{:S(2)}) async-start(s8[8388608]{0:T(1024)(128)(4,1)} %bitcast.119), calls=%async_computation.30 | async-start | bytes 8388608
  506.7 7.6 slice-start.5
  514.4 11.8 %slice-start = ((s8[16777216]{0:T(1024)(128)(4,1)}), s8[4194304]{0:T(1024)(128)(4,1)S(1)}, s32[]{:S(2)}) async-start(s8[16777216]{0:T(1024)(128)(4,1)} %bitcast.117), calls=%async_computation.26 | async-start | bytes 8388608
  514.4 11.8 %slice-start.1 = ((s8[16777216]{0:T(1024)(128)(4,1)}), s8[4194304]{0:T(1024)(128)(4,1)S(1)}, s32[]{:S(2)}) async-start(s8[16777216]{0:T(1024)(128)(4,1)} %bitcast.117), calls=%async_computation.27 | async-start | bytes 8388608
  514.4 11.8 %slice-start.2 = ((s8[16777216]{0:T(1024)(128)(4,1)}), s8[4194304]{0:T(1024)(128)(4,1)S(1)}, s32[]{:S(2)}) async-start(s8[16777216]{0:T(1024)(128)(4,1)} %bitcast.117), calls=%async_computation.28 | async-start | bytes 8388608
  519.3 6.9 slice-start.3
  549.7 4.0 copy-start.9
  549.7 4.0 copy-start.20
  553.7 4.4 copy-start.10
  553.7 4.4 copy-start.16
  553.7 4.4 copy-start.17
  621.4 7.3 copy-start.22
  621.4 7.3 copy-start.24
  621.5 7.3 copy-start.29
  621.5 7.3 copy-start.44
  636.5 267.2 %reduce-scatter.21.cloned.1.call-start = ((), (), s32[]{:S(2)}) async-start(), calls=%async_computation.24 | async-start | bytes 9437184 | tf_op jit(solution)/shard_map/reduce_scatter | solution.py:242
  650.8 405.1 %reduce-scatter.17.cloned.1.call-start = ((), (), s32[]{:S(2)}) async-start(), calls=%async_computation.22 | async-start | bytes 9437184 | tf_op jit(solution)/shard_map/reduce_scatter | solution.py:239
  661.9 90.8 %copy-start.33 = (f32[2,4]{1,0:T(2,128)S(1)}, f32[2,4]{1,0:T(2,128)}, u32[]{:S(2)}) copy-start(f32[2,4]{1,0:T(2,128)} %get-tuple-element.83) | copy-start | bytes 100
  661.9 90.8 %copy-start.34 = (f32[2,4]{1,0:T(2,128)S(1)}, f32[2,4]{1,0:T(2,128)}, u32[]{:S(2)}) copy-start(f32[2,4]{1,0:T(2,128)} %get-tuple-element.81) | copy-start | bytes 100
  661.9 241.9 %copy-start.47 = (f32[1024]{0:T(1024)S(1)}, f32[1024]{0:T(1024)}, u32[]{:S(2)}) copy-start(f32[1024]{0:T(1024)} %param.39) | copy-start | bytes 12292
  661.9 445.6 %reduce-scatter.15.cloned.1.call-start = ((), (), s32[]{:S(2)}) async-start(), calls=%async_computation.21 | async-start | bytes 327680 | tf_op jit(solution)/shard_map/reduce_scatter | solution.py:250
  662.6 446.4 %reduce-scatter.11.cloned.1.call-start = ((), (), s32[]{:S(2)}) async-start(), calls=%async_computation.19 | async-start | bytes 983040 | tf_op jit(solution)/shard_map/reduce_scatter | solution.py:247
  751.9 379.3 %reduce-scatter.23.cloned.1.call-start = ((), (), s32[]{:S(2)}) async-start(), calls=%async_computation.25 | async-start | bytes 1310720 | tf_op jit(solution)/shard_map/reduce_scatter | solution.py:256
  903.7 34.6 %copy-start.19 = (bf16[128,768]{1,0:T(8,128)(2,1)S(1)}, bf16[128,768]{1,0:T(8,128)(2,1)}, u32[]{:S(2)}) copy-start(bf16[128,768]{1,0:T(8,128)(2,1)} %param.30) | copy-start | bytes 589828
  903.8 255.0 %reduce-scatter.19.cloned.1.call-start = ((), (), s32[]{:S(2)}) async-start(), calls=%async_computation.23 | async-start | bytes 1310720 | tf_op jit(solution)/shard_map/reduce_scatter | solution.py:253
  936.7 13.7 %copy-start.48 = (f32[4]{0:T(128)}, f32[4]{0:T(128)S(1)}, u32[]{:S(2)}) copy-start(f32[4]{0:T(128)S(1)} %pmax.7) | copy-start | bytes 52
  1056.0 7.0 copy-start.26
  1056.0 8.1 copy-start.13
  1063.0 1.6 copy-start.4
  1064.6 2.1 copy-start.30
  1064.6 2.1 copy-start.35
  1064.6 2.1 copy-start.36
  (8 other events, 11.1 us)
Sparse Core Ops, SparseCore 0:
  9.6 20.8 all-gather.10
  32.0 16.8 all-gather.14
  51.1 99.0 all-gather.6
  152.2 47.6 all-gather.8
  201.8 123.4 all-gather.12
  327.2 123.0 all-gather.16
  486.9 66.2 reduce-scatter.12
  636.6 115.1 reduce-scatter.8
  755.5 148.1 reduce-scatter.20
  907.6 148.2 reduce-scatter.16
  1058.4 19.0 reduce-scatter.14
  1080.1 23.4 reduce-scatter.10
  1106.1 25.0 reduce-scatter.22
  1133.8 24.9 reduce-scatter.18
where the time goes:
time: 1170 us
  waiting for transfers between devices  725 us (62%)
  blocking collectives  154 us (13%)
  matrix products  153 us (13%)
  local copies, waits for them, and re-layouts  71.4 us (6%)
  other arithmetic  39.2 us (3%)
  between operations  15.3 us (1%)
    reduce_scatter x1, waiting for transfers between devices, body(): lax.psum_scatter(grad_contract.astype(jnp.bfloat16), 'fsdp', scatter_dime...  151 us
    all_gather x1, waiting for transfers between devices, body(): lax.all_gather(partial_full[3], 'fsdp', axis=0, tiled=True)  115 us
    reduce_scatter x1, waiting for transfers between devices, body(): lax.psum_scatter(grad_expand.astype(jnp.bfloat16), 'fsdp', scatter_dimens...  105 us
    all_gather x1, waiting for transfers between devices, body(): lax.all_gather(partial_full[0], 'fsdp', axis=0, tiled=True)  101 us
    reduce_scatter x1, waiting for transfers between devices, body(): lax.psum_scatter(grad_mixing.astype(jnp.bfloat16), 'fsdp', scatter_dimens...  89.2 us
    all_to_all x1, blocking collectives, body(): lax.all_to_all(packed_cot, 'seq', split_axis=1, concat_axis=2, tiled=True)  53.8 us
    all_gather x1, waiting for transfers between devices, body(): lax.all_gather(partial_full[2], 'fsdp', axis=0, tiled=True)  48.9 us
    psum x1, blocking collectives, body(): lax.psum((grad_first_gain, grad_first_shift, grad_mixing_bias, grad_outpu...  40.8 us
  transfers between devices with their start and end apart: 16, of which 12 were waited for; matrix products, arithmetic and copies ran while one was open for 19% of the time, Pallas kernels for 0%

commit v1 on v0

--- a/solution.py
+++ b/solution.py
@@ -7,6 +7,28 @@
 H = 16
 HD = 64
 QBLK = 512
+
+
+def laid_out(pieces, dim):
+    pieces = jnp.moveaxis(pieces, 0, dim)
+    shape = pieces.shape
+    return pieces.reshape(*shape[:dim], shape[dim] * shape[dim + 1], *shape[dim + 2 :])
+
+
+def gather_around(x, axis, dim):
+    length = lax.axis_size(axis)
+    pairs = [(i, (i + 1) % length) for i in range(length)]
+    back = [(b, a) for a, b in pairs]
+    lower, upper = ([], [])
+    for lap in range(length - 1):
+        if lap % 2 == 0:
+            lower.append(lax.ppermute(lower[-1] if lower else x, axis, pairs))
+        else:
+            upper.append(lax.ppermute(upper[-1] if upper else x, axis, back))
+    tiles = jnp.stack([*lower[::-1], x, *upper])
+    shift = lax.axis_index(axis) - len(lower)
+    tiles = tiles[(jnp.arange(length) - shift) % length]
+    return laid_out(tiles, dim)
 
 
 def layer_norm(values, gain, shift):
@@ -153,7 +175,7 @@
     full_weights = (
         lax.all_gather(partial_full[0], "fsdp", axis=0, tiled=True),
         lax.all_gather(partial_full[1], "fsdp", axis=0, tiled=True),
-        lax.all_gather(partial_full[2], "fsdp", axis=0, tiled=True),
+        gather_around(partial_full[2], "fsdp", 0),
         lax.all_gather(partial_full[3], "fsdp", axis=0, tiled=True),
     )
     mixing_full, output_full, expand_full, contract_full = full_weights

time: 1170 us -> 1060 us (0.906)
  waiting for transfers between devices: 725 us -> 588 us
  starting transfers between devices: 9.06 us -> 33.7 us
  blocking collectives: 154 us -> 133 us
  local copies, waits for them, and re-layouts: 71.4 us -> 91.4 us
    ppermute x0 -> x7, waiting for transfers between devices: none -> 175 us  [the longest x4 175 us: gather_around(): lower.append(lax.ppermute(lower[-1] if lower else x, axis, pairs))]
    reduce_scatter x1, waiting for transfers between devices: 151 us -> 31.4 us  [body(): lax.psum_scatter(grad_contract.astype(jnp.bfloat16), 'fsdp', scatter_dime...]
    all_gather x1, waiting for transfers between devices: 101 us -> 0.92 us  [body(): lax.all_gather(partial_full[0], 'fsdp', axis=0, tiled=True)]
    all_gather x1, waiting for transfers between devices: 115 us -> 50.4 us  [body(): lax.all_gather(partial_full[3], 'fsdp', axis=0, tiled=True)]
    all_gather x1 -> x0, waiting for transfers between devices: 48.9 us -> none  [body(): lax.all_gather(partial_full[2], 'fsdp', axis=0, tiled=True)]
    reduce_scatter x1, waiting for transfers between devices: 89.2 us -> 120 us  [body(): lax.psum_scatter(grad_mixing.astype(jnp.bfloat16), 'fsdp', scatter_dimens...]
    ppermute x0 -> x7, starting transfers between devices: none -> 21.2 us  [the longest x3 14.7 us: gather_around(): upper.append(lax.ppermute(upper[-1] if upper else x, axis, back))]
    reduce_scatter x1, waiting for transfers between devices: 0.01 us -> 20.6 us  [body(): lax.psum_scatter(summed_first[0].astype(jnp.bfloat16), 'seq', scatter_dim...]
  transfers between devices with their start and end apart: 16 -> 23, of which waited for: 12 -> 15; matrix products, arithmetic and copies ran while one was open for 19% -> 22% of each run, Pallas kernels for 0% -> 0%
where the time goes in v1:
time: 1060 us; the launch traced here: 1050 us
  waiting for transfers between devices  588 us (55%)
  matrix products  151 us (14%)
  blocking collectives  133 us (13%)
  local copies, waits for them, and re-layouts  91.4 us (9%)
  other arithmetic  40.4 us (4%)
  starting transfers between devices  33.7 us (3%)
  between operations  15.6 us (1%)
    ppermute x4, waiting for transfers between devices, gather_around(): lower.append(lax.ppermute(lower[-1] if lower else x, axis, pairs))  175 us
    reduce_scatter x1, waiting for transfers between devices, body(): lax.psum_scatter(grad_mixing.astype(jnp.bfloat16), 'fsdp', scatter_dimens...  120 us
    reduce_scatter x1, waiting for transfers between devices, body(): lax.psum_scatter(grad_expand.astype(jnp.bfloat16), 'fsdp', scatter_dimens...  106 us
    all_to_all x1, blocking collectives, body(): lax.all_to_all(packed_cot, 'seq', split_axis=1, concat_axis=2, tiled=True)  53.9 us
    all_gather x1, waiting for transfers between devices, body(): lax.all_gather(partial_full[3], 'fsdp', axis=0, tiled=True)  50.4 us
    psum x1, blocking collectives, body(): lax.psum((grad_first_gain, grad_first_shift, grad_mixing_bias, grad_outpu...  40.8 us
    unnamed x155, local copies, waits for them, and re-layouts  34.2 us
    reduce_scatter x1, waiting for transfers between devices, body(): lax.psum_scatter(grad_contract.astype(jnp.bfloat16), 'fsdp', scatter_dime...  31.4 us
  transfers between devices with their start and end apart: 23, of which 15 were waited for; matrix products, arithmetic and copies ran while one was open for 22% of the time, Pallas kernels for 0%

profile of v1, /device:TPU:0, one launch (start us, length us, event | category | flops | bytes accessed | tf_op | source)
XLA Modules:
  0.0 1053.4 jit_solution(10702376058551517211)
XLA Ops:
  8.7 11.7 %all_gather.21 = bf16[128,3072]{1,0:T(8,128)(2,1)} all-gather(bf16[128,768]{1,0:T(8,128)(2,1)} %param.30), channel_id=1, replica_groups=mesh['fsdp'=8,'seq'=4] {'seq'}, dimensions={1}, use_global_device_ids=true | all-gather | bytes 983040 | tf_op jit(solution)/shard_map/all_gather | solution.py:170
  20.5 8.6 all-gather.10.cloned.1.call-done
  30.5 6.5 all_gather.23
  37.1 20.2 %collective-permute-done = bf16[128,4096]{1,0:T(8,128)(2,1)S(1)} collective-permute-done((bf16[128,4096]{1,0:T(8,128)(2,1)}, bf16[128,4096]{1,0:T(8,128)(2,1)S(1)}, u32[]{:S(2)}, u32[]{:S(2)}) %collective-permute-start) | collective-permute-done | bytes 1048608 | tf_op jit(solution)/shard_map/ppermute | solution.py:25
  57.3 4.7 collective-permute-start.4
  62.0 48.5 %collective-permute-done.1 = bf16[128,4096]{1,0:T(8,128)(2,1)} collective-permute-done((bf16[128,4096]{1,0:T(8,128)(2,1)S(1)}, bf16[128,4096]{1,0:T(8,128)(2,1)}, u32[]{:S(2)}, u32[]{:S(2)}) %collective-permute-start.1) | collective-permute-done | bytes 1048608 | tf_op jit(solution)/shard_map/ppermute | solution.py:25
  110.4 2.6 collective-permute-start.2
  115.3 64.4 %collective-permute-done.2 = bf16[128,4096]{1,0:T(8,128)(2,1)} collective-permute-done((bf16[128,4096]{1,0:T(8,128)(2,1)}, bf16[128,4096]{1,0:T(8,128)(2,1)}, u32[]{:S(2)}, u32[]{:S(2)}) %collective-permute-start.2) | collective-permute-done | bytes 1048608 | tf_op jit(solution)/shard_map/ppermute | solution.py:25
  179.7 2.5 collective-permute-start.3
  185.9 7.8 collective-permute-start.6
  193.7 42.1 %collective-permute-done.3 = bf16[128,4096]{1,0:T(8,128)(2,1)} collective-permute-done((bf16[128,4096]{1,0:T(8,128)(2,1)}, bf16[128,4096]{1,0:T(8,128)(2,1)}, u32[]{:S(2)}, u32[]{:S(2)}) %collective-permute-start.3) | collective-permute-done | bytes 1048608 | tf_op jit(solution)/shard_map/ppermute | solution.py:25
  244.8 7.8 add_convert_fusion
  252.6 3.2 copy.155
  257.6 4.2 all-to-all-start
  268.6 30.0 %all-to-all-done = bf16[2,256,16,192]{1,3,0,2:T(8,128)(2,1)S(1)} async-done(((bf16[2,256,16,192]{1,3,0,2:T(8,128)(2,1)}), bf16[2,256,16,192]{1,3,0,2:T(8,128)(2,1)S(1)}, u32[]{:S(2)}, u32[]{:S(2)}) %all-to-all-start) | async-done | bytes 3145760 | tf_op jit(solution)/shard_map/all_to_all | solution.py:192
  298.7 4.1 copy.158
  302.7 4.9 all_to_all.51
  310.6 3.1 copy-done.9
  314.1 3.0 fusion.102
  317.1 3.4 fusion
  323.2 5.2 fusion.69
  328.4 2.7 fusion.70
  332.7 2.7 reshape.370
  335.3 4.2 all-to-all-start.1
  342.0 8.7 gather_fusion
  350.7 3.4 all-to-all-done.1
  354.1 3.1 reshape.371
  357.2 2.6 copy.162
  359.9 3.4 fusion.104
  364.2 7.0 fusion.92
  371.2 50.4 %all-gather.14.cloned.1.call-done = bf16[4096,1024]{1,0:T(8,128)(2,1)} async-done(((bf16[512,1024]{1,0:T(8,128)(2,1)}), bf16[4096,1024]{1,0:T(8,128)(2,1)}) %all-gather.14.cloned.1.call-update) | async-done | bytes 8388624 | tf_op jit(solution)/shard_map/all_gather | solution.py:179
  421.6 13.9 %convert_reduce_fusion = (f32[4096]{0:T(1024)}, bf16[2,256,4096]{2,1,0:T(8,128)(2,1)S(1)}) fusion(f32[2,256,4096]{2,1,0:T(8,128)} %fusion.92, f32[4096]{0:T(1024)S(1)} %copy-done.58, bf16[2,256,1024]{2,1,0:T(8,128)(2,1)} %param.40, bf16[4096,1024]{1,0:T(8,128)(2,1)} %all-gather.14.cloned.1.call-done), kind=kOutput, calls=%fused_computation.26 | convolution fusion | flops 4343197696 | bytes 22052864 | tf_op jit(solution)/shard_map/ntd,id->nti/dot_general | solution.py:215
  435.5 9.8 multiply_reduce_fusion.2
  447.8 2.6 bitcast_convert_fusion.3
  450.5 13.0 %bitcast_convert_fusion = bf16[4096,1024]{1,0:T(8,128)(2,1)} fusion(bf16[2,256,1024]{2,1,0:T(8,128)(2,1)S(1)} %copy-done.16, f32[2,256,4096]{2,1,0:T(8,128)} %fusion.92, f32[4096]{0:T(1024)S(1)} %copy-done.58), kind=kOutput, calls=%fused_computation.1 | convolution fusion | flops 4320133120 | bytes 17842176 | tf_op jit(solution)/shard_map/nti,ntd->id/dot_general | solution.py:213
  465.2 3.5 fusion.53
  471.3 3.5 all-to-all-start.2
  475.5 13.7 %all-to-all-done.2 = bf16[2,256,16,64]{1,3,0,2:T(8,128)(2,1)S(1)} async-done(((bf16[2,256,16,64]{1,3,0,2:T(8,128)(2,1)}), bf16[2,256,16,64]{1,3,0,2:T(8,128)(2,1)S(1)}, u32[]{:S(2)}, u32[]{:S(2)}) %all-to-all-start.2) | async-done | bytes 1048608 | tf_op jit(solution)/shard_map/all_to_all | solution.py:239
  491.3 8.5 fusion.98
  500.7 5.0 multiply_convert_fusion.1
  505.7 3.5 fusion.67
  509.2 3.6 fusion.61
  512.8 2.4 fusion.58
  515.2 10.9 %fusion.97 = (f32[2,4]{1,0:T(2,128)}, f32[2,4,512]{2,1,0:T(4,128)}, f32[2,4,512,1024]{3,2,1,0:T(8,128)}) fusion(f32[2,4,512,1024]{3,2,1,0:T(8,128)S(1)} %bitcast.134, f32[2,4,512]{2,1,0:T(4,128)} %bitcast.155, bf16[2,1024,4,192]{1,3,2,0:T(8,128)(2,1)} %copy-done.8, bf16[2,1024,4,64]{1,3,2,0:T(8,128)(2,1)} %copy-done.10), kind=kOutput, calls=%fused_computation.155 | convolution fusion | flops 553644032 | bytes 35160096 | tf_op jit(solution)/shard_map/nqhd,nkhd->nhqk/dot_general | solution.py:117
  526.1 8.0 multiply_convert_fusion
  534.2 3.6 fusion.44
  537.8 4.8 fusion.68
  542.6 4.4 fusion.43
  548.8 7.6 copy.170
  556.4 53.9 %all_to_all.66 = bf16[2,1024,4,192]{3,2,0,1:T(4,128)(2,1)} all-to-all(bf16[2,1024,4,192]{3,2,0,1:T(4,128)(2,1)} %copy.170), channel_id=1, replica_groups=mesh['fsdp'=8,'seq'=4] {'seq'}, dimensions={1} | all-to-all | bytes 6291456 | tf_op jit(solution)/shard_map/all_to_all | solution.py:241
  610.3 7.3 copy.172
  617.6 7.8 bitcast_convert_fusion.2
  627.0 9.3 bitcast_convert_fusion.1
  637.0 31.4 %reduce-scatter.21.cloned.1.call-done = bf16[512,1024]{1,0:T(8,128)(2,1)} async-done(((bf16[4096,1024]{1,0:T(8,128)(2,1)}), bf16[512,1024]{1,0:T(8,128)(2,1)}) %reduce-scatter.21.cloned.1.call-update) | async-done | bytes 1048592 | tf_op jit(solution)/shard_map/reduce_scatter | solution.py:264
  669.1 120.2 %reduce-scatter.9.cloned.1.call-done = bf16[128,3072]{1,0:T(8,128)(2,1)} async-done(((bf16[1024,3072]{1,0:T(8,128)(2,1)}), bf16[128,3072]{1,0:T(8,128)(2,1)}) %reduce-scatter.9.cloned.1.call-update) | async-done | bytes 786448 | tf_op jit(solution)/shard_map/reduce_scatter | solution.py:255
  789.4 12.2 %add_convert_fusion.1 = bf16[2,256,1024]{2,1,0:T(8,128)(2,1)} fusion(f32[2,256,1024]{2,1,0:T(8,128)S(1)} %copy-done.7, bf16[4096,1024]{1,0:T(8,128)(2,1)} %all-gather.14.cloned.1.call-done, f32[1024]{0:T(1024)S(1)} %copy-done.64, f32[2,256,4096]{2,1,0:T(8,128)} %fusion.92, f32[4096]{0:T(1024)S(1)} %copy-done.59), kind=kOutput, calls=%fused_computation.80 | convolution fusion | flops 4317511680 | bytes 19943424 | tf_op jit(solution)/shard_map/nti,id->ntd/dot_general | solution.py:208
  801.7 20.6 %pmax.7 = f32[4]{0:T(128)S(1)} all-reduce(f32[4]{0:T(128)S(1)} %maximum_reduce_fusion), channel_id=1, replica_groups=mesh['fsdp'=8,'seq'=4] {'fsdp'}, use_global_device_ids=true, to_apply=%region_41.42 | all-reduce | flops 4 | bytes 32 | tf_op jit(solution)/shard_map/pmax | solution.py:295
  824.7 7.9 copy.193
  832.6 3.4 convert_reduce_fusion.1
  836.3 105.5 %reduce-scatter.17.cloned.1.call-done = bf16[128,4096]{1,0:T(8,128)(2,1)} async-done(((bf16[1024,4096]{1,0:T(8,128)(2,1)}), bf16[128,4096]{1,0:T(8,128)(2,1)}) %reduce-scatter.17.cloned.1.call-update) | async-done | bytes 1048592 | tf_op jit(solution)/shard_map/reduce_scatter | solution.py:261
  941.9 7.0 fusion.99
  952.6 40.8 %all-reduce.2 = (f32[1024]{0:T(1024)}, f32[1024]{0:T(1024)}, f32[3072]{0:T(1024)}, f32[1024]{0:T(1024)}, f32[1024]{0:T(1024)}, /*index=5*/f32[1024]{0:T(1024)}, f32[4096]{0:T(1024)}, f32[1024]{0:T(1024)}) all-reduce(f32[1024]{0:T(1024)S(1)} %get-tuple-element.87, ...), channel_id=1, replica_groups=mesh['fsdp'=8,'seq'=4] {'fsdp','seq'}, use_global_device_ids=true, to_apply=%region_15.16 | all-reduce | flops 13312 | bytes 106496 | tf_op jit(solution)/shard_map/psum | solution.py:282
  996.6 20.6 %reduce-scatter.11.cloned.1.call-done = bf16[128,768]{1,0:T(8,128)(2,1)} async-done(((bf16[128,3072]{1,0:T(8,128)(2,1)}), bf16[128,768]{1,0:T(8,128)(2,1)}) %reduce-scatter.11.cloned.1.call-update) | async-done | bytes 196624 | tf_op jit(solution)/shard_map/reduce_scatter | solution.py:269
  1019.0 25.9 %reduce-scatter.19.cloned.1.call-done = bf16[128,1024]{1,0:T(8,128)(2,1)} async-done(((bf16[128,4096]{1,0:T(8,128)(2,1)}), bf16[128,1024]{1,0:T(8,128)(2,1)}) %reduce-scatter.19.cloned.1.call-update) | async-done | bytes 262160 | tf_op jit(solution)/shard_map/reduce_scatter | solution.py:275
  (240 shorter events, 65.4 us)
Async XLA Ops:
  7.2 176.5 %copy-start.2 = (bf16[2,256,1024]{2,1,0:T(8,128)(2,1)S(1)}, bf16[2,256,1024]{2,1,0:T(8,128)(2,1)}, u32[]{:S(2)}) copy-start(bf16[2,256,1024]{2,1,0:T(8,128)(2,1)} %param.27) | copy-start | bytes 3145732
  7.2 21.9 %all-gather.10.cloned.1.call-start = ((), (), s32[]{:S(2)}) async-start(), calls=%async_computation.14 | async-start | bytes 1310720 | tf_op jit(solution)/shard_map/all_gather | solution.py:172
  7.9 177.9 %all-gather.12.cloned.1.call-start = ((), (), s32[]{:S(2)}) async-start(), calls=%async_computation.15 | async-start | bytes 1310720 | tf_op jit(solution)/shard_map/all_gather | solution.py:173
  8.7 236.1 %all-gather.6.cloned.1.call-start = ((), (), s32[]{:S(2)}) async-start(), calls=%async_computation.12 | async-start | bytes 7077888 | tf_op jit(solution)/shard_map/all_gather | solution.py:176
  20.4 339.4 %all-gather.8.cloned.1.call-start = ((), (), s32[]{:S(2)}) async-start(), calls=%async_computation.13 | async-start | bytes 2359296 | tf_op jit(solution)/shard_map/all_gather | solution.py:177
  29.1 28.2 %collective-permute-start = (bf16[128,4096]{1,0:T(8,128)(2,1)}, bf16[128,4096]{1,0:T(8,128)(2,1)S(1)}, u32[]{:S(2)}, u32[]{:S(2)}) collective-permute-start(bf16[128,4096]{1,0:T(8,128)(2,1)} %all-gather.10.cloned.1.call-done), channel_id=1, source_target_pairs={{0,4},{4,8},{8,12},{12,16},{16,20},{20,24},{24,28},{28,0},{1,5},{5... | collective-permute-start | bytes 3145736 | tf_op jit(solution)/shard_map/ppermute | solution.py:25
  37.0 384.6 %all-gather.14.cloned.1.call-start = ((), (), s32[]{:S(2)}) async-start(), calls=%async_computation.16 | async-start | bytes 9437184 | tf_op jit(solution)/shard_map/all_gather | solution.py:179
  57.3 53.2 %collective-permute-start.1 = (bf16[128,4096]{1,0:T(8,128)(2,1)S(1)}, bf16[128,4096]{1,0:T(8,128)(2,1)}, u32[]{:S(2)}, u32[]{:S(2)}) collective-permute-start(bf16[128,4096]{1,0:T(8,128)(2,1)S(1)} %collective-permute-done), channel_id=1, source_target_pairs={{0,4},{4,8},{8,12},{12,16},{16,20},{20,24},{24,28},{28,0},{1,5},{5... | collective-permute-start | bytes 3145736 | tf_op jit(solution)/shard_map/ppermute | solution.py:25
  57.3 55.9 %collective-permute-start.4 = (bf16[128,4096]{1,0:T(8,128)(2,1)}, bf16[128,4096]{1,0:T(8,128)(2,1)S(1)}, u32[]{:S(2)}, u32[]{:S(2)}) collective-permute-start(bf16[128,4096]{1,0:T(8,128)(2,1)} %all-gather.10.cloned.1.call-done), channel_id=1, source_target_pairs={{4,0},{8,4},{12,8},{16,12},{20,16},{24,20},{28,24},{0,28},{5,1},{9... | collective-permute-start | bytes 3145736 | tf_op jit(solution)/shard_map/ppermute | solution.py:27
  110.4 69.3 %collective-permute-start.2 = (bf16[128,4096]{1,0:T(8,128)(2,1)}, bf16[128,4096]{1,0:T(8,128)(2,1)}, u32[]{:S(2)}, u32[]{:S(2)}) collective-permute-start(bf16[128,4096]{1,0:T(8,128)(2,1)} %collective-permute-done.1), channel_id=1, source_target_pairs={{0,4},{4,8},{8,12},{12,16},{16,20},{20,24},{24,28},{28,0},{1,5},{5... | collective-permute-start | bytes 3145736 | tf_op jit(solution)/shard_map/ppermute | solution.py:25
  113.1 129.6 %copy-start.24 = (bf16[128,4096]{1,0:T(8,128)(2,1)}, bf16[128,4096]{1,0:T(8,128)(2,1)S(1)}, u32[]{:S(2)}) copy-start(bf16[128,4096]{1,0:T(8,128)(2,1)S(1)} %collective-permute-done.4) | copy-start | bytes 3145732
  113.2 72.8 %collective-permute-start.5 = (bf16[128,4096]{1,0:T(8,128)(2,1)S(1)}, bf16[128,4096]{1,0:T(8,128)(2,1)}, u32[]{:S(2)}, u32[]{:S(2)}) collective-permute-start(bf16[128,4096]{1,0:T(8,128)(2,1)S(1)} %collective-permute-done.4), channel_id=1, source_target_pairs={{4,0},{8,4},{12,8},{16,12},{20,16},{24,20},{28,24},{0,28},{5,1},{9... | collective-permute-start | bytes 3145736 | tf_op jit(solution)/shard_map/ppermute | solution.py:27
  179.7 56.1 %collective-permute-start.3 = (bf16[128,4096]{1,0:T(8,128)(2,1)}, bf16[128,4096]{1,0:T(8,128)(2,1)}, u32[]{:S(2)}, u32[]{:S(2)}) collective-permute-start(bf16[128,4096]{1,0:T(8,128)(2,1)} %collective-permute-done.2), channel_id=1, source_target_pairs={{0,4},{4,8},{8,12},{12,16},{16,20},{20,24},{24,28},{28,0},{1,5},{5... | collective-permute-start | bytes 3145736 | tf_op jit(solution)/shard_map/ppermute | solution.py:25
  183.7 61.1 %copy-start.39 = (f32[2,256]{1,0:T(2,128)}, f32[2,256]{1,0:T(2,128)S(1)}, u32[]{:S(2)}) copy-start(f32[2,256]{1,0:T(2,128)S(1)} %broadcast_multiply_fusion.1) | copy-start | bytes 6148
  184.7 60.1 %copy-start.41 = (f32[2,256]{1,0:T(2,128)}, f32[2,256]{1,0:T(2,128)S(1)}, u32[]{:S(2)}) copy-start(f32[2,256]{1,0:T(2,128)S(1)} %fusion.93) | copy-start | bytes 6148
  185.9 58.9 %copy-start.46 = (f32[1024]{0:T(1024)S(1)}, f32[1024]{0:T(1024)}, u32[]{:S(2)}) copy-start(f32[1024]{0:T(1024)} %param.28) | copy-start | bytes 12292
  185.9 58.9 %copy-start.57 = (f32[3072]{0:T(1024)S(1)}, f32[3072]{0:T(1024)}, u32[]{:S(2)}) copy-start(f32[3072]{0:T(1024)} %param.31) | copy-start | bytes 36868
  185.9 58.9 %copy-start.60 = (f32[1024]{0:T(1024)S(1)}, f32[1024]{0:T(1024)}, u32[]{:S(2)}) copy-start(f32[1024]{0:T(1024)} %param.29) | copy-start | bytes 12292
  185.9 153.7 %collective-permute-start.6 = (bf16[128,4096]{1,0:T(8,128)(2,1)}, bf16[128,4096]{1,0:T(8,128)(2,1)}, u32[]{:S(2)}, u32[]{:S(2)}) collective-permute-start(bf16[128,4096]{1,0:T(8,128)(2,1)} %collective-permute-done.5), channel_id=1, source_target_pairs={{4,0},{8,4},{12,8},{16,12},{20,16},{24,20},{28,24},{0,28},{5,1},{9... | collective-permute-start | bytes 3145736 | tf_op jit(solution)/shard_map/ppermute | solution.py:27
  257.6 41.1 %all-to-all-start = ((bf16[2,256,16,192]{1,3,0,2:T(8,128)(2,1)}), bf16[2,256,16,192]{1,3,0,2:T(8,128)(2,1)S(1)}, u32[]{:S(2)}, u32[]{:S(2)}) async-start(bf16[2,256,16,192]{1,3,0,2:T(8,128)(2,1)} %copy.156), calls=%async_computation | async-start | bytes 6291456 | tf_op jit(solution)/shard_map/all_to_all | solution.py:192
  309.4 19.0 %copy-start.1 = (f32[2,4,512,512]{2,3,1,0:T(8,128)}, f32[2,4,512,512]{2,3,1,0:T(8,128)S(1)}, u32[]{:S(2)}) copy-start(f32[2,4,512,512]{2,3,1,0:T(8,128)S(1)} %get-tuple-element.109) | copy-start | bytes 25165828
  309.4 19.0 %copy-start.31 = (f32[2,4,512]{2,1,0:T(4,128)}, f32[2,4,512]{2,1,0:T(4,128)S(1)}, u32[]{:S(2)}) copy-start(f32[2,4,512]{2,1,0:T(4,128)S(1)} %get-tuple-element.108) | copy-start | bytes 49156
  314.1 14.3 %copy-start.33 = (f32[2,4,512]{2,1,0:T(4,128)}, f32[2,4,512]{2,1,0:T(4,128)S(1)}, u32[]{:S(2)}) copy-start(f32[2,4,512]{2,1,0:T(4,128)S(1)} %fusion.17) | copy-start | bytes 49156
  335.3 18.8 %all-to-all-start.1 = ((bf16[4,2,65536]{2,1,0:T(2,128)(2,1)}), bf16[4,2,65536]{2,1,0:T(2,128)(2,1)}, u32[]{:S(2)}, u32[]{:S(2)}) async-start(bf16[4,2,65536]{2,1,0:T(2,128)(2,1)} %reshape.370), calls=%async_computation.1 | async-start | bytes 2097152 | tf_op jit(solution)/shard_map/all_to_all | solution.py:99
  339.6 296.8 %reduce-scatter.13.cloned.1.call-start = ((), (), s32[]{:S(2)}) async-start(), calls=%async_computation.19 | async-start | bytes 2359296 | tf_op jit(solution)/shard_map/reduce_scatter | solution.py:258
  350.7 9.1 copy-start.3
  350.7 9.1 copy-start.45
  363.3 82.1 %copy-start.6 = (f32[2,256,1024]{2,1,0:T(8,128)}, f32[2,256,1024]{2,1,0:T(8,128)S(1)}, u32[]{:S(2)}) copy-start(f32[2,256,1024]{2,1,0:T(8,128)S(1)} %get-tuple-element.111) | copy-start | bytes 6291460
  363.7 81.7 %copy-start.49 = (f32[2,256]{1,0:T(2,128)}, f32[2,256]{1,0:T(2,128)S(1)}, u32[]{:S(2)}) copy-start(f32[2,256]{1,0:T(2,128)S(1)} %fusion.94) | copy-start | bytes 6148
  364.2 57.4 %copy-start.58 = (f32[4096]{0:T(1024)S(1)}, f32[4096]{0:T(1024)}, u32[]{:S(2)}) copy-start(f32[4096]{0:T(1024)} %param.37) | copy-start | bytes 49156
  435.5 9.8 copy-start.66
  450.5 217.9 %reduce-scatter.21.cloned.1.call-start = ((), (), s32[]{:S(2)}) async-start(), calls=%async_computation.23 | async-start | bytes 9437184 | tf_op jit(solution)/shard_map/reduce_scatter | solution.py:264
  468.7 6.2 copy-start.34
  468.7 6.2 copy-start.36
  468.7 6.2 copy-start.38
  471.3 18.0 %all-to-all-start.2 = ((bf16[2,256,16,64]{1,3,0,2:T(8,128)(2,1)}), bf16[2,256,16,64]{1,3,0,2:T(8,128)(2,1)S(1)}, u32[]{:S(2)}, u32[]{:S(2)}) async-start(bf16[2,256,16,64]{1,3,0,2:T(8,128)(2,1)} %copy.165), calls=%async_computation.2 | async-start | bytes 2097152 | tf_op jit(solution)/shard_map/all_to_all | solution.py:239
  474.8 314.5 %reduce-scatter.9.cloned.1.call-start = ((), (), s32[]{:S(2)}) async-start(), calls=%async_computation.17 | async-start | bytes 7077888 | tf_op jit(solution)/shard_map/reduce_scatter | solution.py:255
  474.9 24.9 %copy-start.28 = (f32[1,8,512]{2,1,0:T(8,128)}, f32[1,8,512]{2,1,0:T(8,128)S(1)}, u32[]{:S(2)}) copy-start(f32[1,8,512]{2,1,0:T(8,128)S(1)} %log_add_fusion.1) | copy-start | bytes 49156
  491.2 8.5 copy-start.10
  491.2 8.5 slice-start.4
  491.2 9.4 slice-start.5
  500.7 14.5 %slice-start = ((s8[16777216]{0:T(1024)(128)(4,1)}), s8[4194304]{0:T(1024)(128)(4,1)S(1)}, s32[]{:S(2)}) async-start(s8[16777216]{0:T(1024)(128)(4,1)} %bitcast.133), calls=%async_computation.25 | async-start | bytes 8388608
  500.7 14.5 %slice-start.1 = ((s8[16777216]{0:T(1024)(128)(4,1)}), s8[4194304]{0:T(1024)(128)(4,1)S(1)}, s32[]{:S(2)}) async-start(s8[16777216]{0:T(1024)(128)(4,1)} %bitcast.133), calls=%async_computation.26 | async-start | bytes 8388608
  500.7 14.5 %slice-start.2 = ((s8[16777216]{0:T(1024)(128)(4,1)}), s8[4194304]{0:T(1024)(128)(4,1)S(1)}, s32[]{:S(2)}) async-start(s8[16777216]{0:T(1024)(128)(4,1)} %bitcast.133), calls=%async_computation.27 | async-start | bytes 8388608
  505.7 7.1 copy-start.11
  505.7 7.1 copy-start.29
  526.1 8.1 copy-start.19
  610.3 7.3 copy-start.40
  610.3 7.3 copy-start.42
  610.3 7.3 copy-start.47
  610.3 7.3 copy-start.61
  625.5 316.3 %reduce-scatter.17.cloned.1.call-start = ((), (), s32[]{:S(2)}) async-start(), calls=%async_computation.21 | async-start | bytes 9437184 | tf_op jit(solution)/shard_map/reduce_scatter | solution.py:261
  636.3 32.8 %copy-start.51 = (f32[2,4]{1,0:T(2,128)S(1)}, f32[2,4]{1,0:T(2,128)}, u32[]{:S(2)}) copy-start(f32[2,4]{1,0:T(2,128)} %get-tuple-element.83) | copy-start | bytes 100
  636.3 32.8 %copy-start.52 = (f32[2,4]{1,0:T(2,128)S(1)}, f32[2,4]{1,0:T(2,128)}, u32[]{:S(2)}) copy-start(f32[2,4]{1,0:T(2,128)} %get-tuple-element.81) | copy-start | bytes 100
  636.3 153.1 %copy-start.59 = (f32[4096]{0:T(1024)S(1)}, f32[4096]{0:T(1024)}, u32[]{:S(2)}) copy-start(f32[4096]{0:T(1024)} %param.37) | copy-start | bytes 49156
  636.3 153.1 %copy-start.64 = (f32[1024]{0:T(1024)S(1)}, f32[1024]{0:T(1024)}, u32[]{:S(2)}) copy-start(f32[1024]{0:T(1024)} %param.39) | copy-start | bytes 12292
  636.3 357.0 %reduce-scatter.15.cloned.1.call-start = ((), (), s32[]{:S(2)}) async-start(), calls=%async_computation.20 | async-start | bytes 327680 | tf_op jit(solution)/shard_map/reduce_scatter | solution.py:272
  636.9 358.0 %reduce-scatter.23.cloned.1.call-start = ((), (), s32[]{:S(2)}) async-start(), calls=%async_computation.24 | async-start | bytes 1310720 | tf_op jit(solution)/shard_map/reduce_scatter | solution.py:278
  668.3 348.9 %reduce-scatter.11.cloned.1.call-start = ((), (), s32[]{:S(2)}) async-start(), calls=%async_computation.18 | async-start | bytes 983040 | tf_op jit(solution)/shard_map/reduce_scatter | solution.py:269
  789.3 34.6 %copy-start.25 = (bf16[128,768]{1,0:T(8,128)(2,1)S(1)}, bf16[128,768]{1,0:T(8,128)(2,1)}, u32[]{:S(2)}) copy-start(bf16[128,768]{1,0:T(8,128)(2,1)} %param.30) | copy-start | bytes 589828
  789.4 255.5 %reduce-scatter.19.cloned.1.call-start = ((), (), s32[]{:S(2)}) async-start(), calls=%async_computation.22 | async-start | bytes 1310720 | tf_op jit(solution)/shard_map/reduce_scatter | solution.py:275
  822.2 13.8 %copy-start.65 = (f32[4]{0:T(128)}, f32[4]{0:T(128)S(1)}, u32[]{:S(2)}) copy-start(f32[4]{0:T(128)S(1)} %pmax.7) | copy-start | bytes 52
  941.8 7.0 copy-start.44
  941.8 8.1 copy-start.17
  (32 other events, 106.1 us)
Sparse Core Ops, SparseCore 0:
  9.6 19.4 all-gather.9
  30.6 16.8 all-gather.11
  49.7 195.0 all-gather.5
  246.7 49.4 all-gather.7
  298.2 123.4 all-gather.13
  450.6 66.0 reduce-scatter.12
  520.3 147.9 reduce-scatter.20
  672.3 116.9 reduce-scatter.8
  793.4 148.3 reduce-scatter.16
  944.1 19.1 reduce-scatter.14
  965.9 25.2 reduce-scatter.22
  993.6 23.6 reduce-scatter.10
  1019.9 24.8 reduce-scatter.18
